TPU v7x, 512 devices: a whole 4x8x8 slice. The times are simulated.
512 devices in a mesh: shard: 64 (over x, z, core), tensor: 8 (over y).
Axes of the slice: x: 4, y: 8, z: 8, core: 2. Of those that a mesh axis runs over, the one named last changes fastest.
Arguments:
- grad: float32 [8, 512, 1024], P(None, 'shard', 'tensor'), may hold values from -500 to 500
- momentum: float32 [8, 512, 1024], P(None, 'shard', 'tensor'), may hold values from -6 to 6
- weight: float32 [8, 512, 1024], P(None, 'shard', 'tensor'), may hold values from -0.625 to 0.625
Outputs:
- new_weight: float32 [8, 512, 1024], P(None, 'shard', 'tensor')
- new_momentum: float32 [8, 512, 1024], P(None, 'shard', 'tensor')
- update: float32 [8, 512, 1024], P(None, 'shard', 'tensor')
All inputs are finite; a program needn't handle non-finite values.
Results may differ from a plain program's by a relative error of at most 0.0078.
Values may be sent and summed in bfloat16 or wider, within the bound.
A program may use at most 64 MiB of HBM per device.

v0:
```python
import math
import jax
import jax.numpy as jnp
from jax import lax
from jax.sharding import PartitionSpec as P

ITERS = 3
mu_decay = 0.95
learn_rate = 0.05
weight_decay = 0.1
update_gain = 0.2
first_coef = 3.4445
second_coef = -4.775
third_coef = 2.0315
epsilon = 1e-07


def polish(iterate, gram):
    wide = iterate.astype(jnp.float32)
    squared = jnp.dot(gram, gram, precision=lax.Precision.HIGHEST)
    poly = second_coef * gram + third_coef * squared
    mixed = jnp.dot(poly, wide, precision=lax.Precision.HIGHEST)
    fresh = first_coef * wide + mixed
    return fresh.astype(jnp.bfloat16)


def on_device(grad, momentum, weight):
    mats, rows_local, cols_local = grad.shape
    n_tensor = lax.axis_size("tensor")
    new_momentum = mu_decay * momentum + grad
    advance = (grad + mu_decay * new_momentum).astype(jnp.bfloat16)
    mine = lax.all_to_all(advance, "tensor", split_axis=0, concat_axis=2, tiled=True)
    whole = lax.all_gather(mine, "shard", axis=1, tiled=True)[0]
    wide = whole.astype(jnp.float32)
    frob = jnp.sqrt(jnp.sum(wide * wide)) + epsilon
    iterate = (wide / frob).astype(jnp.bfloat16)
    for step in range(ITERS):
        gram = jnp.dot(iterate, iterate.T, preferred_element_type=jnp.float32)
        iterate = polish(iterate, gram)
    start = lax.axis_index("shard") * rows_local
    rows = lax.dynamic_slice_in_dim(iterate, start, rows_local, axis=0)
    ortho = lax.all_to_all(rows[None], "tensor", split_axis=2, concat_axis=0, tiled=True)
    width = cols_local * n_tensor
    update = update_gain * math.sqrt(width) * ortho.astype(jnp.float32)
    new_weight = weight - learn_rate * (update + weight_decay * weight)
    return (new_weight, new_momentum, update)


def solution(mesh):
    in_specs = (P(None, "shard", "tensor"), P(None, "shard", "tensor"), P(None, "shard", "tensor"))
    out_specs = (P(None, "shard", "tensor"), P(None, "shard", "tensor"), P(None, "shard", "tensor"))
    return jax.shard_map(
        on_device, mesh=mesh, in_specs=in_specs, out_specs=out_specs, check_vma=False
    )
```

profile of v0, /device:TPU:1, one launch (start us, length us, event | category | flops | bytes accessed | tf_op | source)
XLA Modules:
  0.0 151.1 jit_solution(5558221943511022706)
XLA Ops:
  7.2 0.0 all-gather.2.cloned.1.call-start
  7.2 1.4 add_convert_fusion.2
  8.6 14.2 %all_to_all.27 = bf16[8,8,128]{2,1,0:T(8,128)(2,1)} all-to-all(bf16[8,8,128]{2,1,0:T(8,128)(2,1)S(1)} %get-tuple-element.3), channel_id=1, replica_groups=mesh['shard'=64,'tensor'=8] {'tensor'}, dimensions={0} | all-to-all | bytes 32768 | tf_op jit(solution)/shard_map/all_to_all | solution.py:32
  22.8 0.0 all-gather.2.cloned.1.call-update
  22.8 84.4 %all-gather.2.cloned.1.call-done = bf16[1,512,1024]{2,1,0:T(8,128)(2,1)} async-done(((bf16[1,8,1024]{2,1,0:T(8,128)(2,1)}), bf16[1,512,1024]{2,1,0:T(8,128)(2,1)}) %all-gather.2.cloned.1.call-update) | async-done | bytes 1048592 | tf_op jit(solution)/shard_map/all_gather | solution.py:33
  107.2 2.4 %fusion = f32[]{:T(128)} fusion(bf16[1,512,1024]{2,1,0:T(8,128)(2,1)} %all-gather.2.cloned.1.call-done), kind=kLoop, calls=%fused_computation.2 | loop fusion | flops 1572863 | bytes 1048580 | tf_op jit(solution)/shard_map/reduce_sum | solution.py:35
  110.2 2.3 %fusion.8 = f32[512,512]{1,0:T(8,128)S(1)} fusion(bf16[1,512,1024]{2,1,0:T(8,128)(2,1)} %all-gather.2.cloned.1.call-done, f32[]{:T(128)S(6)} %add.35), kind=kOutput, calls=%fused_computation.20 | convolution fusion | flops 538443776 | bytes 2097156 | tf_op jit(solution)/shard_map/dot_general | solution.py:38
  112.5 1.9 %fusion.4 = f32[512,512]{1,0:T(8,128)S(1)} fusion(f32[512,512]{1,0:T(8,128)S(1)} %fusion.8), kind=kOutput, calls=%fused_computation.11 | convolution fusion | flops 1611399168 | bytes 2097152 | tf_op jit(solution)/shard_map/dot_general | solution.py:20
  114.5 1.9 %add_convert_fusion.1 = bf16[512,1024]{1,0:T(8,128)(2,1)S(1)} fusion(f32[512,512]{1,0:T(8,128)S(1)} %fusion.4, f32[]{:T(128)S(6)} %add.35, bf16[1,512,1024]{2,1,0:T(8,128)(2,1)S(1)} %copy-done), kind=kOutput, calls=%fused_computation.5 | convolution fusion | flops 3226468352 | bytes 3145732 | tf_op jit(solution)/shard_map/dot_general | solution.py:22
  116.4 0.7 fusion.11
  117.1 1.9 %fusion.3 = f32[512,512]{1,0:T(8,128)S(1)} fusion(f32[512,512]{1,0:T(8,128)S(1)} %fusion.11), kind=kOutput, calls=%fused_computation.9 | convolution fusion | flops 1611399168 | bytes 2097152 | tf_op jit(solution)/shard_map/dot_general | solution.py:20
  119.1 1.9 %add_convert_fusion = bf16[512,1024]{1,0:T(8,128)(2,1)S(1)} fusion(bf16[512,1024]{1,0:T(8,128)(2,1)S(1)} %add_convert_fusion.1, f32[512,512]{1,0:T(8,128)S(1)} %fusion.3), kind=kOutput, calls=%fused_computation.4 | convolution fusion | flops 3223322624 | bytes 3145728 | tf_op jit(solution)/shard_map/dot_general | solution.py:22
  120.9 0.7 fusion.12
  121.7 1.9 %fusion.2 = f32[512,512]{1,0:T(8,128)S(1)} fusion(f32[512,512]{1,0:T(8,128)S(1)} %fusion.12), kind=kOutput, calls=%fused_computation.7 | convolution fusion | flops 1611399168 | bytes 2097152 | tf_op jit(solution)/shard_map/dot_general | solution.py:20
  123.6 2.0 %fusion.13 = f32[512,1024]{1,0:T(8,128)S(1)} fusion(f32[512,512]{1,0:T(8,128)S(1)} %fusion.2, bf16[512,1024]{1,0:T(8,128)(2,1)S(1)} %add_convert_fusion), kind=kOutput, calls=%fused_computation.23 | convolution fusion | flops 3221225472 | bytes 4194304 | tf_op jit(solution)/shard_map/dot_general | solution.py:22
  125.7 0.4 copy.7
  126.1 0.5 broadcast.39
  126.6 2.3 %reduce.1 = bf16[1024,8]{1,0:T(8,128)(2,1)S(1)} reduce(bf16[1024,1,8]{2,1,0:T(2,128)(2,1)S(1)} %bitcast.37, bf16[]{:T(256)} %broadcast.39), dimensions={1}, to_apply=%bitcast.18.reduce_sub_computation | reduce | bytes 32770
  128.8 0.3 reshape.19
  129.1 12.9 %all_to_all.28 = bf16[8,2,512]{2,1,0:T(2,128)(2,1)S(1)} all-to-all(bf16[8,2,512]{2,1,0:T(2,128)(2,1)S(1)} %reshape.19), channel_id=1, replica_groups=mesh['shard'=64,'tensor'=8] {'tensor'}, dimensions={0} | all-to-all | bytes 32768 | tf_op jit(solution)/shard_map/all_to_all | solution.py:42
  142.0 0.7 reshape.20
  142.7 0.7 convert_multiply_fusion.1
  143.4 0.2 copy.8
  143.6 0.6 multiply_subtract_fusion
  (7 shorter events, 0.0 us)
Async XLA Ops:
  7.2 100.0 %all-gather.2.cloned.1.call-start = ((), (), s32[]{:S(2)}) async-start(), calls=%async_computation.2 | async-start | bytes 1064960 | tf_op jit(solution)/shard_map/all_gather | solution.py:33
  112.5 1.9 %copy-start = (bf16[1,512,1024]{2,1,0:T(8,128)(2,1)S(1)}, bf16[1,512,1024]{2,1,0:T(8,128)(2,1)}, u32[]{:S(2)}) copy-start(bf16[1,512,1024]{2,1,0:T(8,128)(2,1)} %all-gather.2.cloned.1.call-done) | copy-start | bytes 3145732
  125.6 18.0 %copy-start.2 = (f32[8,8,128]{2,1,0:T(8,128)S(1)}, f32[8,8,128]{2,1,0:T(8,128)}, u32[]{:S(2)}) copy-start(f32[8,8,128]{2,1,0:T(8,128)} %param.5) | copy-start | bytes 98308
  143.6 0.6 copy-start.1
Sparse Core Ops, SparseCore 0:
  22.9 84.2 all-gather.1
where the time goes:
time: 151 us
  waiting for transfers between devices  84.4 us (56%)
  blocking collectives  27 us (18%)
  matrix products  15.3 us (10%)
  between operations  14.9 us (10%)
  other arithmetic  7.41 us (5%)
  local copies, waits for them, and re-layouts  2.04 us (1%)
    all_gather x1, waiting for transfers between devices, on_device(): whole = lax.all_gather(mine, 'shard', axis=1, tiled=True)[0]  84.4 us
    all_to_all x1, blocking collectives, on_device(): lax.all_to_all(advance, 'tensor', split_axis=0, concat_axis=2, tiled=True)  14.2 us
    all_to_all x1, blocking collectives, on_device(): lax.all_to_all(rows[None], 'tensor', split_axis=2, concat_axis=0, tiled=T...  12.9 us
    dot_general x3, matrix products, polish(): mixed = jnp.dot(poly, wide, precision=lax.Precision.HIGHEST)  5.81 us
    dot_general x3, matrix products, polish(): squared = jnp.dot(gram, gram, precision=lax.Precision.HIGHEST)  5.73 us
    dot_general x3, matrix products, on_device(): gram = jnp.dot(iterate, iterate.T, preferred_element_type=jnp.float32)  3.78 us
  transfers between devices with their start and end apart: 1, of which 1 were waited for; matrix products, arithmetic and copies ran while one was open for 0% of the time, Pallas kernels for 0%

commit v1 on v0

--- a/solution.py
+++ b/solution.py
@@ -1,3 +1,4 @@
+import functools
 import math
 import jax
 import jax.numpy as jnp
@@ -15,6 +16,16 @@
 epsilon = 1e-07
 
 
+def process_unit(mine_x, d0, dim_no):
+    x_next = lax.axis_size("tensor")
+    view_out = jnp.split(mine_x, x_next, axis=d0)
+    reached = lax.all_to_all(jnp.stack(view_out, axis=0), "tensor", 0, 0)
+    return jnp.concatenate(reached, axis=dim_no)
+
+
+scan_face = functools.partial(process_unit, d0=0, dim_no=2)
+
+
 def polish(iterate, gram):
     wide = iterate.astype(jnp.float32)
     squared = jnp.dot(gram, gram, precision=lax.Precision.HIGHEST)
@@ -29,7 +40,7 @@
     n_tensor = lax.axis_size("tensor")
     new_momentum = mu_decay * momentum + grad
     advance = (grad + mu_decay * new_momentum).astype(jnp.bfloat16)
-    mine = lax.all_to_all(advance, "tensor", split_axis=0, concat_axis=2, tiled=True)
+    mine = scan_face(advance)
     whole = lax.all_gather(mine, "shard", axis=1, tiled=True)[0]
     wide = whole.astype(jnp.float32)
     frob = jnp.sqrt(jnp.sum(wide * wide)) + epsilon

time: 151 us -> 151 us (level)
  no operation moved by 1% of the time
where the time goes in v1:
time: 151 us
  waiting for transfers between devices  84.4 us (56%)
  blocking collectives  27 us (18%)
  matrix products  15.3 us (10%)
  between operations  14.9 us (10%)
  other arithmetic  7.41 us (5%)
  local copies, waits for them, and re-layouts  2.09 us (1%)
    all_gather x1, waiting for transfers between devices, on_device(): whole = lax.all_gather(mine, 'shard', axis=1, tiled=True)[0]  84.4 us
    all_to_all x1, blocking collectives, process_unit(): reached = lax.all_to_all(jnp.stack(view_out, axis=0), 'tensor', 0, 0)  14.2 us
    all_to_all x1, blocking collectives, on_device(): lax.all_to_all(rows[None], 'tensor', split_axis=2, concat_axis=0, tiled=T...  12.9 us
    dot_general x3, matrix products, polish(): mixed = jnp.dot(poly, wide, precision=lax.Precision.HIGHEST)  5.81 us
    dot_general x3, matrix products, polish(): squared = jnp.dot(gram, gram, precision=lax.Precision.HIGHEST)  5.73 us
    dot_general x3, matrix products, on_device(): gram = jnp.dot(iterate, iterate.T, preferred_element_type=jnp.float32)  3.78 us
  transfers between devices with their start and end apart: 1, of which 1 were waited for; matrix products, arithmetic and copies ran while one was open for 0% of the time, Pallas kernels for 0%

profile of v1, /device:TPU:1, one launch (start us, length us, event | category | flops | bytes accessed | tf_op | source)
XLA Modules:
  0.0 151.2 jit_solution(14741303369283499735)
XLA Ops:
  7.2 0.0 all-gather.2.cloned.1.call-start
  7.2 1.4 add_convert_fusion.2
  8.7 14.2 %all_to_all.14 = bf16[8,1,8,128]{3,2,1,0:T(8,128)(2,1)} all-to-all(bf16[8,1,8,128]{3,2,1,0:T(8,128)(2,1)S(1)} %constant_dynamic-update-slice_fusion), channel_id=1, replica_groups=mesh['shard'=64,'tensor'=8] {'tensor'}, dimensions={0} | all-to-all | bytes 32768 | tf_op jit(solution)/shard_map/all_to_all | solution.py:22
  22.8 0.0 all-gather.2.cloned.1.call-update
  22.9 84.4 %all-gather.2.cloned.1.call-done = bf16[1,512,1024]{2,1,0:T(8,128)(2,1)} async-done(((bf16[1,8,1024]{2,1,0:T(8,128)(2,1)}), bf16[1,512,1024]{2,1,0:T(8,128)(2,1)}) %all-gather.2.cloned.1.call-update) | async-done | bytes 1048592 | tf_op jit(solution)/shard_map/all_gather | solution.py:44
  107.2 2.4 %fusion = f32[]{:T(128)} fusion(bf16[1,512,1024]{2,1,0:T(8,128)(2,1)} %all-gather.2.cloned.1.call-done), kind=kLoop, calls=%fused_computation.2 | loop fusion | flops 1572863 | bytes 1048580 | tf_op jit(solution)/shard_map/reduce_sum | solution.py:46
  110.3 2.3 %fusion.8 = f32[512,512]{1,0:T(8,128)S(1)} fusion(bf16[1,512,1024]{2,1,0:T(8,128)(2,1)} %all-gather.2.cloned.1.call-done, f32[]{:T(128)S(6)} %add.35), kind=kOutput, calls=%fused_computation.36 | convolution fusion | flops 538443776 | bytes 2097156 | tf_op jit(solution)/shard_map/dot_general | solution.py:49
  112.6 1.9 %fusion.4 = f32[512,512]{1,0:T(8,128)S(1)} fusion(f32[512,512]{1,0:T(8,128)S(1)} %fusion.8), kind=kOutput, calls=%fused_computation.11 | convolution fusion | flops 1611399168 | bytes 2097152 | tf_op jit(solution)/shard_map/dot_general | solution.py:31
  114.5 1.9 %add_convert_fusion.1 = bf16[512,1024]{1,0:T(8,128)(2,1)S(1)} fusion(f32[512,512]{1,0:T(8,128)S(1)} %fusion.4, f32[]{:T(128)S(6)} %add.35, bf16[1,512,1024]{2,1,0:T(8,128)(2,1)S(1)} %copy-done), kind=kOutput, calls=%fused_computation.5 | convolution fusion | flops 3226468352 | bytes 3145732 | tf_op jit(solution)/shard_map/dot_general | solution.py:33
  116.5 0.7 fusion.11
  117.2 1.9 %fusion.3 = f32[512,512]{1,0:T(8,128)S(1)} fusion(f32[512,512]{1,0:T(8,128)S(1)} %fusion.11), kind=kOutput, calls=%fused_computation.9 | convolution fusion | flops 1611399168 | bytes 2097152 | tf_op jit(solution)/shard_map/dot_general | solution.py:31
  119.1 1.9 %add_convert_fusion = bf16[512,1024]{1,0:T(8,128)(2,1)S(1)} fusion(bf16[512,1024]{1,0:T(8,128)(2,1)S(1)} %add_convert_fusion.1, f32[512,512]{1,0:T(8,128)S(1)} %fusion.3), kind=kOutput, calls=%fused_computation.4 | convolution fusion | flops 3223322624 | bytes 3145728 | tf_op jit(solution)/shard_map/dot_general | solution.py:33
  121.0 0.7 fusion.12
  121.8 1.9 %fusion.2 = f32[512,512]{1,0:T(8,128)S(1)} fusion(f32[512,512]{1,0:T(8,128)S(1)} %fusion.12), kind=kOutput, calls=%fused_computation.7 | convolution fusion | flops 1611399168 | bytes 2097152 | tf_op jit(solution)/shard_map/dot_general | solution.py:31
  123.7 2.0 %fusion.13 = f32[512,1024]{1,0:T(8,128)S(1)} fusion(f32[512,512]{1,0:T(8,128)S(1)} %fusion.2, bf16[512,1024]{1,0:T(8,128)(2,1)S(1)} %add_convert_fusion), kind=kOutput, calls=%fused_computation.39 | convolution fusion | flops 3221225472 | bytes 4194304 | tf_op jit(solution)/shard_map/dot_general | solution.py:33
  125.7 0.4 copy.7
  126.1 0.5 broadcast.39
  126.7 2.3 %reduce.1 = bf16[1024,8]{1,0:T(8,128)(2,1)S(1)} reduce(bf16[1024,1,8]{2,1,0:T(2,128)(2,1)S(1)} %bitcast.67, bf16[]{:T(256)} %broadcast.39), dimensions={1}, to_apply=%bitcast.48.reduce_sub_computation | reduce | bytes 32770
  128.9 0.3 reshape.27
  129.2 12.9 %all_to_all.15 = bf16[8,2,512]{2,1,0:T(2,128)(2,1)S(1)} all-to-all(bf16[8,2,512]{2,1,0:T(2,128)(2,1)S(1)} %reshape.27), channel_id=1, replica_groups=mesh['shard'=64,'tensor'=8] {'tensor'}, dimensions={0} | all-to-all | bytes 32768 | tf_op jit(solution)/shard_map/all_to_all | solution.py:53
  142.1 0.7 reshape.28
  142.8 0.7 convert_multiply_fusion.1
  143.5 0.2 copy.8
  143.7 0.6 multiply_subtract_fusion
  (15 shorter events, 0.1 us)
Async XLA Ops:
  7.2 100.1 %all-gather.2.cloned.1.call-start = ((), (), s32[]{:S(2)}) async-start(), calls=%async_computation.2 | async-start | bytes 1064960 | tf_op jit(solution)/shard_map/all_gather | solution.py:44
  112.6 1.9 %copy-start = (bf16[1,512,1024]{2,1,0:T(8,128)(2,1)S(1)}, bf16[1,512,1024]{2,1,0:T(8,128)(2,1)}, u32[]{:S(2)}) copy-start(bf16[1,512,1024]{2,1,0:T(8,128)(2,1)} %all-gather.2.cloned.1.call-done) | copy-start | bytes 3145732
  125.7 18.0 %copy-start.2 = (f32[8,8,128]{2,1,0:T(8,128)S(1)}, f32[8,8,128]{2,1,0:T(8,128)}, u32[]{:S(2)}) copy-start(f32[8,8,128]{2,1,0:T(8,128)} %param.5) | copy-start | bytes 98308
  143.7 0.6 copy-start.1
Sparse Core Ops, SparseCore 0:
  23.0 84.2 all-gather.1
